TPU v7x, 32 devices: a whole 2x2x4 slice. The times are simulated.
32 devices in a mesh: fsdp: 32 (over z, y, x, core).
Axes of the slice: x: 2, y: 2, z: 4, core: 2. Of those that a mesh axis runs over, the one named last changes fastest.
Arguments:
- inputs: bfloat16 [6144, 1280], P('fsdp'), may hold values from -6 to 6
- ln1_gain: float32 [1280], P('fsdp'), may hold values from 0.5 to 1.5
- ln1_bias: float32 [1280], P('fsdp'), may hold values from -1 to 1
- w_query: float32 [1280, 1280], P('fsdp'), may hold values from -0.3125 to 0.3125
- b_query: float32 [1280], P('fsdp'), may hold values from -2.5 to 2.5
- w_key: float32 [1280, 1280], P('fsdp'), may hold values from -0.15625 to 0.15625
- w_value: float32 [1280, 1280], P('fsdp'), may hold values from -0.15625 to 0.15625
- b_value: float32 [1280], P('fsdp'), may hold values from -2.5 to 2.5
- w_out: float32 [1280, 1280], P('fsdp'), may hold values from -0.625 to 0.625
- b_out: float32 [1280], P('fsdp'), may hold values from -2.5 to 2.5
- ln2_gain: float32 [1280], P('fsdp'), may hold values from 0.5 to 1.5
- ln2_bias: float32 [1280], P('fsdp'), may hold values from -1 to 1
- w_up: float32 [1280, 5120], P('fsdp'), may hold values from -0.15625 to 0.15625
- b_up: float32 [5120], P('fsdp'), may hold values from -2.5 to 2.5
- w_down: float32 [5120, 1280], P('fsdp'), may hold values from -0.078125 to 0.078125
- b_down: float32 [1280], P('fsdp'), may hold values from -2.5 to 2.5
- lengths: int32 [4], replicated, may hold values from 1153 to 1536, as said below
- cotangent: bfloat16 [6144, 1280], P('fsdp'), may hold values from -6 to 6
Outputs:
- output: float32 [6144, 1280], P('fsdp')
- grad_inputs: float32 [6144, 1280], P('fsdp')
- grad_ln1_gain: float32 [1280], P('fsdp')
- grad_ln1_bias: float32 [1280], P('fsdp')
- grad_w_query: float32 [1280, 1280], P('fsdp')
- grad_b_query: float32 [1280], P('fsdp')
- grad_w_key: float32 [1280, 1280], P('fsdp')
- grad_w_value: float32 [1280, 1280], P('fsdp')
- grad_b_value: float32 [1280], P('fsdp')
- grad_w_out: float32 [1280, 1280], P('fsdp')
- grad_b_out: float32 [1280], P('fsdp')
- grad_ln2_gain: float32 [1280], P('fsdp')
- grad_ln2_bias: float32 [1280], P('fsdp')
- grad_w_up: float32 [1280, 5120], P('fsdp')
- grad_b_up: float32 [5120], P('fsdp')
- grad_w_down: float32 [5120, 1280], P('fsdp')
- grad_b_down: float32 [1280], P('fsdp')
Inputs may be any that keep to these rules, and one draw needn't show every extreme that they name: Frames of clip c at positions lengths[c] and beyond are padding; some clip has exactly 1536 real frames and some exactly 1153.
All inputs are finite; a program needn't handle non-finite values.
Results may differ from a plain program's by a relative error of at most 0.014.
The roundings to bfloat16 on the way count: a program that leaves them out, or rounds other values in their place, can miss the bound.
Values may be sent and summed in bfloat16 or wider, within the bound.
A program may use at most 320 MiB of HBM per device.

v0:
```python
import math
import jax
import jax.numpy as jnp
from jax import lax
from jax.sharding import PartitionSpec as P

D = 1280
H = 16
HD = 80
CLIP_LEN = 1536
epsilon = 1e-05
masked_value = -1e30


def swapped(block, axis, bit):
    count = lax.axis_size(axis)
    route = []
    for low in range(count):
        high = low | 1 << bit
        if high != low and high < count:
            route += [(low, high), (high, low)]
    return lax.ppermute(block, axis, route)


def layer_norm(values, gain, offset):
    average = jnp.mean(values, axis=-1, keepdims=True)
    centred = values - average
    variance = jnp.mean(centred * centred, axis=-1, keepdims=True)
    return centred * lax.rsqrt(variance + epsilon) * gain + offset


def norm_backward(values, gain, grad_out):

    def normalize(values_in, gain_in):
        return layer_norm(values_in, gain_in, 0.0)

    unused, pullback = jax.vjp(normalize, values, gain)
    grad_values, grad_gain = pullback(grad_out)
    return (grad_values, grad_gain, jnp.sum(grad_out, axis=0))


def gelu_exact(values):
    return jax.nn.gelu(values, approximate=False)


def matmul(left, right):
    return jnp.dot(left, right, preferred_element_type=jnp.float32)


def outer_sum(left, right):
    return lax.dot_general(
        left, right, (((0,), (0,)), ((), ())), preferred_element_type=jnp.float32
    )


def times_transposed(left, right):
    return lax.dot_general(
        left, right, (((1,), (1,)), ((), ())), preferred_element_type=jnp.float32
    )


def column_sums(matrix):
    return jnp.sum(matrix.astype(jnp.float32), axis=0)


def split_heads(matrix):
    return matrix.reshape(matrix.shape[0], H, HD).transpose(1, 0, 2)


def merge_heads(stacked):
    return stacked.transpose(1, 0, 2).reshape(stacked.shape[1], H * HD)


def on_device(
    inputs,
    ln1_gain,
    ln1_bias,
    w_query,
    b_query,
    w_key,
    w_value,
    b_value,
    w_out,
    b_out,
    ln2_gain,
    ln2_bias,
    w_up,
    b_up,
    w_down,
    b_down,
    lengths,
    cotangent,
):
    (
        whole_ln1_gain,
        whole_ln1_bias,
        whole_w_query,
        whole_b_query,
        whole_w_key,
        whole_w_value,
        whole_b_value,
        whole_w_out,
        whole_b_out,
        whole_ln2_gain,
        whole_ln2_bias,
        whole_w_up,
        whole_b_up,
        whole_w_down,
        whole_b_down,
    ) = (
        lax.all_gather(ln1_gain.astype(jnp.bfloat16), "fsdp", axis=0, tiled=True),
        lax.all_gather(ln1_bias.astype(jnp.bfloat16), "fsdp", axis=0, tiled=True),
        lax.all_gather(w_query.astype(jnp.bfloat16), "fsdp", axis=0, tiled=True),
        lax.all_gather(b_query.astype(jnp.bfloat16), "fsdp", axis=0, tiled=True),
        lax.all_gather(w_key.astype(jnp.bfloat16), "fsdp", axis=0, tiled=True),
        lax.all_gather(w_value.astype(jnp.bfloat16), "fsdp", axis=0, tiled=True),
        lax.all_gather(b_value.astype(jnp.bfloat16), "fsdp", axis=0, tiled=True),
        lax.all_gather(w_out.astype(jnp.bfloat16), "fsdp", axis=0, tiled=True),
        lax.all_gather(b_out.astype(jnp.bfloat16), "fsdp", axis=0, tiled=True),
        lax.all_gather(ln2_gain.astype(jnp.bfloat16), "fsdp", axis=0, tiled=True),
        lax.all_gather(ln2_bias.astype(jnp.bfloat16), "fsdp", axis=0, tiled=True),
        lax.all_gather(w_up.astype(jnp.bfloat16), "fsdp", axis=0, tiled=True),
        lax.all_gather(b_up.astype(jnp.bfloat16), "fsdp", axis=0, tiled=True),
        lax.all_gather(w_down.astype(jnp.bfloat16), "fsdp", axis=0, tiled=True),
        lax.all_gather(b_down.astype(jnp.bfloat16), "fsdp", axis=0, tiled=True),
    )
    device_index = lax.axis_index("fsdp")
    row_count = inputs.shape[0]
    group_size = CLIP_LEN // row_count
    levels = group_size.bit_length() - 1
    length = lengths[device_index // group_size]
    key_valid = (jnp.arange(CLIP_LEN, dtype=jnp.int32) < length)[None, :]
    score_scale = 1.0 / math.sqrt(HD)
    source = inputs.astype(jnp.float32)
    normed = layer_norm(
        source, whole_ln1_gain.astype(jnp.float32), whole_ln1_bias.astype(jnp.float32)
    ).astype(jnp.bfloat16)
    query_rows = (matmul(normed, whole_w_query) + whole_b_query.astype(jnp.float32)).astype(
        jnp.bfloat16
    )
    key_rows = matmul(normed, whole_w_key).astype(jnp.bfloat16)
    value_rows = (matmul(normed, whole_w_value) + whole_b_value.astype(jnp.float32)).astype(
        jnp.bfloat16
    )
    key_all, value_all = (key_rows, value_rows)
    for bit_number in range(levels):
        other_key, other_value = swapped((key_all, value_all), "fsdp", bit_number)
        upper_half = device_index // (1 << bit_number) % 2 == 1
        key_all = jnp.where(
            upper_half,
            jnp.concatenate([other_key, key_all], axis=0),
            jnp.concatenate([key_all, other_key], axis=0),
        )
        value_all = jnp.where(
            upper_half,
            jnp.concatenate([other_value, value_all], axis=0),
            jnp.concatenate([value_all, other_value], axis=0),
        )

    def head_scores(query_head, key_head):
        scores = times_transposed(query_head, key_head) * score_scale
        return jnp.where(key_valid, scores, masked_value)

    def head_forward(operands):
        query_head, key_head, value_head = operands
        masked = head_scores(query_head, key_head)
        largest = jnp.max(masked, axis=-1, keepdims=True)
        exponent = jnp.exp(masked - largest)
        total = jnp.sum(exponent, axis=-1, keepdims=True)
        attn_weights = (exponent / total).astype(jnp.bfloat16)
        return (matmul(attn_weights, value_head), (largest + jnp.log(total))[:, 0])

    query_heads = split_heads(query_rows)
    key_heads = split_heads(key_all)
    value_heads = split_heads(value_all)
    mixed_heads, log_totals = lax.map(head_forward, (query_heads, key_heads, value_heads))
    attended = merge_heads(mixed_heads).astype(jnp.bfloat16)
    residual = source + (matmul(attended, whole_w_out) + whole_b_out.astype(jnp.float32))
    normed_two = layer_norm(
        residual, whole_ln2_gain.astype(jnp.float32), whole_ln2_bias.astype(jnp.float32)
    ).astype(jnp.bfloat16)
    hidden = matmul(normed_two, whole_w_up) + whole_b_up.astype(jnp.float32)
    activated = gelu_exact(hidden).astype(jnp.bfloat16)
    output = residual + (matmul(activated, whole_w_down) + whole_b_down.astype(jnp.float32))
    (
        back_w_query,
        back_w_key,
        back_w_value,
        back_w_out,
        back_w_up,
        back_w_down,
        back_ln1_gain,
        back_ln2_gain,
    ) = (
        lax.all_gather(w_query.astype(jnp.bfloat16), "fsdp", axis=0, tiled=True),
        lax.all_gather(w_key.astype(jnp.bfloat16), "fsdp", axis=0, tiled=True),
        lax.all_gather(w_value.astype(jnp.bfloat16), "fsdp", axis=0, tiled=True),
        lax.all_gather(w_out.astype(jnp.bfloat16), "fsdp", axis=0, tiled=True),
        lax.all_gather(w_up.astype(jnp.bfloat16), "fsdp", axis=0, tiled=True),
        lax.all_gather(w_down.astype(jnp.bfloat16), "fsdp", axis=0, tiled=True),
        lax.all_gather(ln1_gain.astype(jnp.bfloat16), "fsdp", axis=0, tiled=True),
        lax.all_gather(ln2_gain.astype(jnp.bfloat16), "fsdp", axis=0, tiled=True),
    )
    grad_b_down = column_sums(cotangent)
    grad_activated = times_transposed(cotangent, back_w_down)
    unused, gelu_pullback = jax.vjp(gelu_exact, hidden)
    grad_hidden = gelu_pullback(grad_activated)[0].astype(jnp.bfloat16)
    shard_w_down = lax.psum_scatter(
        outer_sum(activated, cotangent), "fsdp", scatter_dimension=0, tiled=True
    )
    grad_b_up = column_sums(grad_hidden)
    grad_normed_two = times_transposed(grad_hidden, back_w_up)
    grad_from_second, grad_ln2_gain, grad_ln2_bias = norm_backward(
        residual, back_ln2_gain.astype(jnp.float32), grad_normed_two
    )
    grad_residual = cotangent.astype(jnp.float32) + grad_from_second
    grad_branch = grad_residual.astype(jnp.bfloat16)
    grad_b_out = column_sums(grad_branch)
    grad_attended = times_transposed(grad_branch, back_w_out).astype(jnp.bfloat16)

    def head_backward(operands):
        query_head, key_head, value_head, grad_head, log_total = operands
        masked = head_scores(query_head, key_head)
        attn_weights = jnp.exp(masked - log_total[:, None])
        grad_weights = times_transposed(grad_head, value_head)
        inner = jnp.sum(attn_weights * grad_weights, axis=-1, keepdims=True)
        grad_scores = (attn_weights * (grad_weights - inner)).astype(jnp.bfloat16)
        grad_query = matmul(grad_scores, key_head) * score_scale
        grad_key = outer_sum(grad_scores, query_head) * score_scale
        grad_value = outer_sum(attn_weights.astype(jnp.bfloat16), grad_head)
        return (grad_query, grad_key, grad_value)

    grad_query_heads, grad_key_heads, grad_value_heads = lax.map(
        head_backward, (query_heads, key_heads, value_heads, split_heads(grad_attended), log_totals)
    )
    grad_queries = merge_heads(grad_query_heads).astype(jnp.bfloat16)
    grad_key_all = merge_heads(grad_key_heads)
    grad_value_all = merge_heads(grad_value_heads)
    for bit_number in reversed(range(levels)):
        half_rows = grad_key_all.shape[0] // 2
        upper_half = device_index // (1 << bit_number) % 2 == 1
        lower_key, higher_key = (grad_key_all[:half_rows], grad_key_all[half_rows:])
        lower_value, higher_value = (grad_value_all[:half_rows], grad_value_all[half_rows:])
        keep_key = jnp.where(upper_half, higher_key, lower_key)
        send_key = jnp.where(upper_half, lower_key, higher_key)
        keep_value = jnp.where(upper_half, higher_value, lower_value)
        send_value = jnp.where(upper_half, lower_value, higher_value)
        got_key, got_value = (
            swapped(send_key.astype(jnp.bfloat16), "fsdp", bit_number).astype(send_key.dtype),
            swapped(send_value.astype(jnp.bfloat16), "fsdp", bit_number).astype(send_value.dtype),
        )
        grad_key_all = keep_key + got_key
        grad_value_all = keep_value + got_value
    grad_keys = grad_key_all.astype(jnp.bfloat16)
    grad_values = grad_value_all.astype(jnp.bfloat16)
    grad_b_query = column_sums(grad_queries)
    grad_b_value = column_sums(grad_values)
    grad_normed = (
        times_transposed(grad_queries, back_w_query)
        + times_transposed(grad_keys, back_w_key)
        + times_transposed(grad_values, back_w_value)
    )
    grad_from_first, grad_ln1_gain, grad_ln1_bias = norm_backward(
        source, back_ln1_gain.astype(jnp.float32), grad_normed
    )
    grad_inputs = grad_residual + grad_from_first
    stacked = lax.psum_scatter(
        jnp.concatenate(
            [
                jnp.concatenate(
                    [
                        outer_sum(normed, grad_queries),
                        outer_sum(normed, grad_keys),
                        outer_sum(normed, grad_values),
                        outer_sum(attended, grad_branch),
                    ],
                    axis=1,
                ),
                outer_sum(normed_two, grad_hidden),
            ],
            axis=1,
        ),
        "fsdp",
        scatter_dimension=0,
        tiled=True,
    )
    shard_w_up = stacked[:, 4 * D :]
    shard_w_query = stacked[:, 0:D]
    shard_w_key = stacked[:, D : 2 * D]
    shard_w_value = stacked[:, 2 * D : 3 * D]
    shard_w_out = stacked[:, 3 * D : 4 * D]
    (
        shard_ln1_gain,
        shard_ln1_bias,
        shard_b_query,
        shard_b_value,
        shard_b_out,
        shard_ln2_gain,
        shard_ln2_bias,
        shard_b_up,
        shard_b_down,
    ) = (
        lax.psum_scatter(grad_ln1_gain, "fsdp", scatter_dimension=0, tiled=True),
        lax.psum_scatter(grad_ln1_bias, "fsdp", scatter_dimension=0, tiled=True),
        lax.psum_scatter(grad_b_query, "fsdp", scatter_dimension=0, tiled=True),
        lax.psum_scatter(grad_b_value, "fsdp", scatter_dimension=0, tiled=True),
        lax.psum_scatter(grad_b_out, "fsdp", scatter_dimension=0, tiled=True),
        lax.psum_scatter(grad_ln2_gain, "fsdp", scatter_dimension=0, tiled=True),
        lax.psum_scatter(grad_ln2_bias, "fsdp", scatter_dimension=0, tiled=True),
        lax.psum_scatter(grad_b_up, "fsdp", scatter_dimension=0, tiled=True),
        lax.psum_scatter(grad_b_down, "fsdp", scatter_dimension=0, tiled=True),
    )
    return (
        output,
        grad_inputs,
        shard_ln1_gain,
        shard_ln1_bias,
        shard_w_query,
        shard_b_query,
        shard_w_key,
        shard_w_value,
        shard_b_value,
        shard_w_out,
        shard_b_out,
        shard_ln2_gain,
        shard_ln2_bias,
        shard_w_up,
        shard_b_up,
        shard_w_down,
        shard_b_down,
    )


def solution(mesh):
    in_specs = (
        P("fsdp", None),
        P("fsdp"),
        P("fsdp"),
        P("fsdp", None),
        P("fsdp"),
        P("fsdp", None),
        P("fsdp", None),
        P("fsdp"),
        P("fsdp", None),
        P("fsdp"),
        P("fsdp"),
        P("fsdp"),
        P("fsdp", None),
        P("fsdp"),
        P("fsdp", None),
        P("fsdp"),
        P(),
        P("fsdp", None),
    )
    out_specs = (
        P("fsdp", None),
        P("fsdp", None),
        P("fsdp"),
        P("fsdp"),
        P("fsdp", None),
        P("fsdp"),
        P("fsdp", None),
        P("fsdp", None),
        P("fsdp"),
        P("fsdp", None),
        P("fsdp"),
        P("fsdp"),
        P("fsdp"),
        P("fsdp", None),
        P("fsdp"),
        P("fsdp", None),
        P("fsdp"),
    )
    return jax.shard_map(
        on_device, mesh=mesh, in_specs=in_specs, out_specs=out_specs, check_vma=False
    )
```

profile of v0, /device:TPU:14, one launch (start us, length us, event | category | flops | bytes accessed | tf_op | source)
XLA Modules:
  0.0 1651.8 jit_solution(5950444463934327169)
XLA Ops:
  20.4 42.8 %all-reduce.19 = (bf16[1280]{0:T(1024)(128)(2,1)S(1)}, bf16[1280]{0:T(1024)(128)(2,1)S(1)}, bf16[1280]{0:T(1024)(128)(2,1)S(1)}, bf16[1280]{0:T(1024)(128)(2,1)S...) all-reduce(bf16[1280]{0:T(1024)(128)(2,1)S(1)} %dynamic-update-slic, ...), channel_id=1, replica_groups=mesh['fsdp'=32] {'fsdp'}, use_global_device_ids=true, to_apply=%add.2 | all-reduce | flops 15360 | bytes 61440
  63.6 7.3 all-gather.9.cloned.1.call-done
  74.0 58.3 %all-gather.11.cloned.1.call-done = bf16[1280,1280]{1,0:T(8,128)(2,1)} async-done(((bf16[40,1280]{1,0:T(8,128)(2,1)}), bf16[1280,1280]{1,0:T(8,128)(2,1)}) %all-gather.11.cloned.1.call-update) | async-done | bytes 3276816 | tf_op jit(solution)/shard_map/all_gather | solution.py:116
  132.3 2.8 fusion.57
  139.6 22.7 %collective-permute-done.1 = bf16[384,1280]{1,0:T(8,128)(2,1)S(1)} collective-permute-done((bf16[384,1280]{1,0:T(8,128)(2,1)}, bf16[384,1280]{1,0:T(8,128)(2,1)S(1)}, u32[]{:S(2)}, u32[]{:S(2)}) %collective-permute-start.1) | collective-permute-done | bytes 983072 | tf_op jit(solution)/shard_map/ppermute | solution.py:22
  162.3 3.6 maximum_select_fusion.2
  167.7 22.0 %collective-permute-done.4 = bf16[384,1280]{1,0:T(8,128)(2,1)S(1)} collective-permute-done((bf16[384,1280]{1,0:T(8,128)(2,1)S(1)}, bf16[384,1280]{1,0:T(8,128)(2,1)S(1)}, u32[]{:S(2)}, u32[]{:S(2)}) %collective-permute-start.4) | collective-permute-done | bytes 983072 | tf_op jit(solution)/shard_map/ppermute | solution.py:22
  198.9 3.1 all-gather.7.cloned.1.call-done
  202.0 3.6 fusion.56
  212.2 4.4 maximum_select_fusion.7
  220.2 3.4 maximum_select_fusion.3
  224.1 4.0 copy.129
  228.1 5.7 fusion.47
  233.8 7.7 copy.138
  241.5 24.0 %collective-permute-done.5 = bf16[768,1280]{1,0:T(8,128)(2,1)} collective-permute-done((bf16[768,1280]{1,0:T(8,128)(2,1)}, bf16[768,1280]{1,0:T(8,128)(2,1)}, u32[]{:S(2)}, u32[]{:S(2)}) %collective-permute-start.5) | collective-permute-done | bytes 1966112 | tf_op jit(solution)/shard_map/ppermute | solution.py:22
  265.6 4.1 copy.133
  269.7 4.7 fusion.48
  274.3 7.8 copy.139
  282.2 84.0 %while.28 = (s32[]{:T(128)}, bf16[16,192,80]{1,2,0:T(8,128)(2,1)S(1)}, f32[16,192]{1,0:T(8,128)}, bf16[16,192,80]{2,1,0:T(8,128)(2,1)}, bf16[16,1536,80]{2,1,0:T...) while((s32[]{:T(128)}, ...), condition=%wide.region_5.6_spmd.clone, body=%wide.region_2.5_spmd.clone.sunk | while | flops 96732480 | bytes 4469869 | solution.py:176
  366.2 2.9 fusion.85
  369.4 9.5 convolution_add_fusion
  378.8 87.4 %all-gather.17.cloned.1.call-done = bf16[5120,1280]{1,0:T(8,128)(2,1)} async-done(((bf16[160,1280]{1,0:T(8,128)(2,1)}), bf16[5120,1280]{1,0:T(8,128)(2,1)}) %all-gather.17.cloned.1.call-update) | async-done | bytes 13107216 | tf_op jit(solution)/shard_map/all_gather | solution.py:124
  466.2 17.2 %convert_reduce_fusion = (f32[5120]{0:T(1024)S(1)}, bf16[192,5120]{1,0:T(8,128)(2,1)S(1)}, f32[192,5120]{1,0:T(8,128)}) fusion(f32[192,5120]{1,0:T(8,128)} %convolution_add_fusion, bf16[192,1280]{1,0:T(8,128)(2,1)S(1)} %copy-done.7, bf16[5120,1280]{1,0:T(8,128)(2,1)} %all-gather.17.cloned.1.call-done), kind=kOutput, calls=%fused_computation.70 | convolution fusion | flops 2589322240 | bytes 23449600 | tf_op jit(solution)/shard_map/dot_general | solution.py:57
  483.4 10.1 multiply_reduce_fusion.1
  498.2 153.4 %while.29 = (s32[]{:T(128)}, bf16[16,192,80]{1,2,0:T(8,128)(2,1)S(1)}, f32[16,1536,80]{1,2,0:T(8,128)}, f32[16,1536,80]{1,2,0:T(8,128)}, bf16[16,192,80]{2,1,0:T...) while((s32[]{:T(128)}, ...), condition=%wide.region_12.13_spmd.clone, body=%wide.region_10.12_spmd.clone.sunk | while | flops 238723392 | bytes 11284349 | solution.py:233
  651.6 5.2 select_convert_fusion.1
  656.7 4.0 copy.145
  662.1 4.9 select_convert_fusion
  667.0 4.0 copy.147
  671.7 5.8 slice_select_fusion.1
  677.5 5.7 slice_select_fusion
  683.2 5.4 copy.146
  688.6 5.9 copy.148
  694.5 4.0 convolution_dynamic-update-slice_fusion.4
  698.5 8.2 collective-permute-done.6
  710.7 37.5 %collective-permute-done.9 = bf16[768,1280]{1,0:T(8,128)(2,1)} collective-permute-done((bf16[768,1280]{1,0:T(8,128)(2,1)}, bf16[768,1280]{1,0:T(8,128)(2,1)}, u32[]{:S(2)}, u32[]{:S(2)}) %collective-permute-start.9) | collective-permute-done | bytes 1966112 | tf_op jit(solution)/shard_map/ppermute | solution.py:22
  752.4 21.1 %collective-permute-done.10 = bf16[384,1280]{1,0:T(8,128)(2,1)S(1)} collective-permute-done((bf16[384,1280]{1,0:T(8,128)(2,1)S(1)}, bf16[384,1280]{1,0:T(8,128)(2,1)S(1)}, u32[]{:S(2)}, u32[]{:S(2)}) %collective-permute-start.10) | collective-permute-done | bytes 983072 | tf_op jit(solution)/shard_map/ppermute | solution.py:22
  774.3 4.0 convolution_dynamic-update-slice_fusion.3
  778.5 4.0 convolution_dynamic-update-slice_fusion.2
  782.5 3.9 convolution_dynamic-update-slice_fusion.1
  786.3 10.7 convolution_dynamic-update-slice_fusion
  797.1 3.9 multiply_convert_fusion.1
  801.0 11.2 fusion.87
  814.4 3.4 fusion.86
  817.8 8.6 fusion.55
  831.9 47.0 %all-reduce.18 = (f32[1280]{0:T(1024)S(1)}, f32[1280]{0:T(1024)S(1)}, f32[1280]{0:T(1024)S(1)}, f32[1280]{0:T(1024)S(1)}, f32[1280]{0:T(1024)S(1)}, /*index=5*/f...) all-reduce(f32[1280]{0:T(1024)S(1)} %get-tuple-element.224, ...), channel_id=2, replica_groups=mesh['fsdp'=32] {'fsdp'}, use_global_device_ids=true, to_apply=%region_16.17.clone | all-reduce | flops 15360 | bytes 122880
  884.3 472.3 %reduce-scatter.3.cloned.1.call-done = f32[40,10240]{1,0:T(8,128)} async-done(((f32[1280,10240]{1,0:T(8,128)}), f32[40,10240]{1,0:T(8,128)}) %reduce-scatter.3.cloned.1.call-update) | async-done | bytes 1638416 | tf_op jit(solution)/shard_map/reduce_scatter | solution.py:267
  1360.8 284.0 %reduce-scatter.5.cloned.1.call-done = f32[160,1280]{1,0:T(8,128)} async-done(((f32[5120,1280]{1,0:T(8,128)}), f32[160,1280]{1,0:T(8,128)}) %reduce-scatter.5.cloned.1.call-update) | async-done | bytes 819216 | tf_op jit(solution)/shard_map/reduce_scatter | solution.py:208
  (437 shorter events, 312.4 us)
Async XLA Ops:
  7.2 11.0 copy-start.28
  7.2 11.0 copy-start.29
  7.2 11.0 copy-start.30
  7.2 11.0 copy-start.31
  7.2 11.0 copy-start.32
  7.2 11.0 copy-start.33
  7.3 11.0 copy-start.34
  7.3 11.0 copy-start.27
  7.3 11.0 copy-start.35
  7.3 55.9 %copy-start = (bf16[192,1280]{1,0:T(8,128)(2,1)S(1)}, bf16[192,1280]{1,0:T(8,128)(2,1)}, u32[]{:S(2)}) copy-start(bf16[192,1280]{1,0:T(8,128)(2,1)} %param.22) | copy-start | bytes 1474564
  7.3 63.6 %all-gather.9.cloned.1.call-start = ((), (), s32[]{:S(2)}) async-start(), calls=%async_computation.3 | async-start | bytes 3379200 | tf_op jit(solution)/shard_map/all_gather | solution.py:115
  9.0 123.3 %all-gather.11.cloned.1.call-start = ((), (), s32[]{:S(2)}) async-start(), calls=%async_computation.4 | async-start | bytes 3379200 | tf_op jit(solution)/shard_map/all_gather | solution.py:116
  10.7 191.3 %all-gather.7.cloned.1.call-start = ((), (), s32[]{:S(2)}) async-start(), calls=%async_computation.2 | async-start | bytes 3379200 | tf_op jit(solution)/shard_map/all_gather | solution.py:113
  12.3 353.8 %all-gather.13.cloned.1.call-start = ((), (), s32[]{:S(2)}) async-start(), calls=%async_computation.5 | async-start | bytes 3379200 | tf_op jit(solution)/shard_map/all_gather | solution.py:118
  14.0 355.3 %all-gather.15.cloned.1.call-start = ((), (), s32[]{:S(2)}) async-start(), calls=%async_computation.6 | async-start | bytes 13516800 | tf_op jit(solution)/shard_map/all_gather | solution.py:122
  16.0 450.1 %all-gather.17.cloned.1.call-start = ((), (), s32[]{:S(2)}) async-start(), calls=%async_computation.7 | async-start | bytes 13516800 | tf_op jit(solution)/shard_map/all_gather | solution.py:124
  18.1 1338.5 %reduce-scatter.3.cloned.1.call-start = ((), (), s32[]{:S(2)}) async-start(), calls=%async_computation.8 | async-start | bytes 54067200 | tf_op jit(solution)/shard_map/reduce_scatter | solution.py:267
  63.6 71.6 %copy-start.24 = (f32[192]{0:T(256)}, f32[192]{0:T(256)S(1)}, u32[]{:S(2)}) copy-start(f32[192]{0:T(256)S(1)} %fusion.67) | copy-start | bytes 2308
  73.7 64.5 %copy-start.21 = (bf16[192,1280]{1,0:T(8,128)(2,1)}, bf16[192,1280]{1,0:T(8,128)(2,1)S(1)}, u32[]{:S(2)}) copy-start(bf16[192,1280]{1,0:T(8,128)(2,1)S(1)} %convolution_convert_fusion.1) | copy-start | bytes 1474564
  73.7 61.8 %collective-permute-start = (bf16[192,1280]{1,0:T(8,128)(2,1)S(1)}, bf16[192,1280]{1,0:T(8,128)(2,1)S(1)}, u32[]{:S(2)}, u32[]{:S(2)}) collective-permute-start(bf16[192,1280]{1,0:T(8,128)(2,1)S(1)} %convolution_convert_fusion.1), channel_id=1, source_target_pairs={{0,1},{1,0},{2,3},{3,2},{4,5},{5,4},{6,7},{7,6},{8,9},{9,8},{10,11... | collective-permute-start | bytes 1474568 | tf_op jit(solution)/shard_map/ppermute | solution.py:22
  135.2 3.4 copy-start.23
  135.2 3.0 collective-permute-start.3
  135.5 2.7 copy-start.20
  136.7 25.6 %collective-permute-start.1 = (bf16[384,1280]{1,0:T(8,128)(2,1)}, bf16[384,1280]{1,0:T(8,128)(2,1)S(1)}, u32[]{:S(2)}, u32[]{:S(2)}) collective-permute-start(bf16[384,1280]{1,0:T(8,128)(2,1)} %maximum_select_fusion.6), channel_id=1, source_target_pairs={{0,2},{2,0},{1,3},{3,1},{4,6},{6,4},{5,7},{7,5},{8,10},{10,8},{9,1... | collective-permute-start | bytes 2949128 | tf_op jit(solution)/shard_map/ppermute | solution.py:22
  139.0 50.6 %collective-permute-start.4 = (bf16[384,1280]{1,0:T(8,128)(2,1)S(1)}, bf16[384,1280]{1,0:T(8,128)(2,1)S(1)}, u32[]{:S(2)}, u32[]{:S(2)}) collective-permute-start(bf16[384,1280]{1,0:T(8,128)(2,1)S(1)} %maximum_select_fusion.8), channel_id=1, source_target_pairs={{0,2},{2,0},{1,3},{3,1},{4,6},{6,4},{5,7},{7,5},{8,10},{10,8},{9,1... | collective-permute-start | bytes 2949128 | tf_op jit(solution)/shard_map/ppermute | solution.py:22
  139.6 54.5 %copy-start.36 = (s32[4]{0:T(128)S(1)}, s32[4]{0:T(128)}, u32[]{:S(2)}) copy-start(s32[4]{0:T(128)} %param.38) | copy-start | bytes 52
  165.9 58.2 %collective-permute-start.2 = (bf16[768,1280]{1,0:T(8,128)(2,1)}, bf16[768,1280]{1,0:T(8,128)(2,1)}, u32[]{:S(2)}, u32[]{:S(2)}) collective-permute-start(bf16[768,1280]{1,0:T(8,128)(2,1)} %maximum_select_fusion.2), channel_id=1, source_target_pairs={{0,4},{4,0},{1,5},{5,1},{2,6},{6,2},{3,7},{7,3},{8,12},{12,8},{9,1... | collective-permute-start | bytes 5898248 | tf_op jit(solution)/shard_map/ppermute | solution.py:22
  189.7 15.9 copy-start.14
  191.7 73.9 %collective-permute-start.5 = (bf16[768,1280]{1,0:T(8,128)(2,1)}, bf16[768,1280]{1,0:T(8,128)(2,1)}, u32[]{:S(2)}, u32[]{:S(2)}) collective-permute-start(bf16[768,1280]{1,0:T(8,128)(2,1)} %maximum_select_fusion.4), channel_id=1, source_target_pairs={{0,4},{4,0},{1,5},{5,1},{2,6},{6,2},{3,7},{7,3},{8,12},{12,8},{9,1... | collective-permute-start | bytes 5898248 | tf_op jit(solution)/shard_map/ppermute | solution.py:22
  220.2 3.4 copy-start.15
  369.3 96.9 %copy-start.7 = (bf16[192,1280]{1,0:T(8,128)(2,1)S(1)}, bf16[192,1280]{1,0:T(8,128)(2,1)}, u32[]{:S(2)}) copy-start(bf16[192,1280]{1,0:T(8,128)(2,1)} %param.39) | copy-start | bytes 1474564
  483.4 10.1 copy-start.18
  651.6 42.9 %copy-start.6 = (bf16[16,192,80]{1,2,0:T(8,128)(2,1)}, bf16[16,192,80]{1,2,0:T(8,128)(2,1)S(1)}, u32[]{:S(2)}) copy-start(bf16[16,192,80]{1,2,0:T(8,128)(2,1)S(1)} %get-tuple-element.111) | copy-start | bytes 1474564
  660.7 46.0 %collective-permute-start.6 = (bf16[768,1280]{1,0:T(8,128)(2,1)}, bf16[768,1280]{1,0:T(8,128)(2,1)}, u32[]{:S(2)}, u32[]{:S(2)}) collective-permute-start(bf16[768,1280]{1,0:T(8,128)(2,1)} %copy.145), channel_id=1, source_target_pairs={{0,4},{4,0},{1,5},{5,1},{2,6},{6,2},{3,7},{7,3},{8,12},{12,8},{9,1... | collective-permute-start | bytes 5898248 | tf_op jit(solution)/shard_map/ppermute | solution.py:22
  671.0 77.1 %collective-permute-start.9 = (bf16[768,1280]{1,0:T(8,128)(2,1)}, bf16[768,1280]{1,0:T(8,128)(2,1)}, u32[]{:S(2)}, u32[]{:S(2)}) collective-permute-start(bf16[768,1280]{1,0:T(8,128)(2,1)} %copy.147), channel_id=1, source_target_pairs={{0,4},{4,0},{1,5},{5,1},{2,6},{6,2},{3,7},{7,3},{8,12},{12,8},{9,1... | collective-permute-start | bytes 5898248 | tf_op jit(solution)/shard_map/ppermute | solution.py:22
  694.5 12.2 copy-start.2
  706.8 41.4 %copy-start.1 = (f32[768,1280]{1,0:T(8,128)S(1)}, f32[768,1280]{1,0:T(8,128)}, u32[]{:S(2)}) copy-start(f32[768,1280]{1,0:T(8,128)} %copy.148) | copy-start | bytes 11796484
  709.1 42.8 %collective-permute-start.7 = (bf16[384,1280]{1,0:T(8,128)(2,1)S(1)}, bf16[384,1280]{1,0:T(8,128)(2,1)S(1)}, u32[]{:S(2)}, u32[]{:S(2)}) collective-permute-start(bf16[384,1280]{1,0:T(8,128)(2,1)S(1)} %select_convert_fusion.3), channel_id=1, source_target_pairs={{0,2},{2,0},{1,3},{3,1},{4,6},{6,4},{5,7},{7,5},{8,10},{10,8},{9,1... | collective-permute-start | bytes 2949128 | tf_op jit(solution)/shard_map/ppermute | solution.py:22
  750.4 23.1 %collective-permute-start.10 = (bf16[384,1280]{1,0:T(8,128)(2,1)S(1)}, bf16[384,1280]{1,0:T(8,128)(2,1)S(1)}, u32[]{:S(2)}, u32[]{:S(2)}) collective-permute-start(bf16[384,1280]{1,0:T(8,128)(2,1)S(1)} %select_convert_fusion.2), channel_id=1, source_target_pairs={{0,2},{2,0},{1,3},{3,1},{4,6},{6,4},{5,7},{7,5},{8,10},{10,8},{9,1... | collective-permute-start | bytes 2949128 | tf_op jit(solution)/shard_map/ppermute | solution.py:22
  752.3 21.8 %collective-permute-start.8 = (bf16[192,1280]{1,0:T(8,128)(2,1)S(1)}, bf16[192,1280]{1,0:T(8,128)(2,1)S(1)}, u32[]{:S(2)}, u32[]{:S(2)}) collective-permute-start(bf16[192,1280]{1,0:T(8,128)(2,1)S(1)} %select_convert_fusion.5), channel_id=1, source_target_pairs={{0,1},{1,0},{2,3},{3,2},{4,5},{5,4},{6,7},{7,6},{8,9},{9,8},{10,11... | collective-permute-start | bytes 1474568 | tf_op jit(solution)/shard_map/ppermute | solution.py:22
  774.0 4.3 collective-permute-start.11
  774.2 4.0 copy-start.12
  778.5 4.0 copy-start.10
  782.5 3.9 copy-start.19
  797.1 847.7 %reduce-scatter.5.cloned.1.call-start = ((), (), s32[]{:S(2)}) async-start(), calls=%async_computation.9 | async-start | bytes 27033600 | tf_op jit(solution)/shard_map/reduce_scatter | solution.py:208
  797.1 3.9 copy-start.8
  817.8 8.7 copy-start.13
  817.8 8.7 copy-start.16
  (9 other events, 13.3 us)
Sparse Core Ops, SparseCore 0:
  11.5 59.2 all-gather.8
  74.3 57.9 all-gather.10
  135.8 66.1 all-gather.6
  205.3 63.3 all-gather.12
  271.4 95.7 all-gather.14
  369.9 96.2 all-gather.16
  797.2 559.3 reduce-scatter.2
  1359.4 285.2 reduce-scatter.4
where the time goes:
time: 1660 us; the launch traced here: 1650 us
  waiting for transfers between devices  1050 us (63%)
  matrix products  277 us (17%)
  local copies, waits for them, and re-layouts  107 us (6%)
  other arithmetic  102 us (6%)
  blocking collectives  89.8 us (5%)
    reduce_scatter x1, waiting for transfers between devices, on_device(): lax.psum_scatter(jnp.concatenate([jnp.concatenate([outer_sum(normed, grad...  472 us
    reduce_scatter x1, waiting for transfers between devices, on_device(): lax.psum_scatter(outer_sum(activated, cotangent), 'fsdp', scatter_dimensi...  284 us
    ppermute x12, waiting for transfers between devices, swapped(): return lax.ppermute(block, axis, route)  136 us
    dot_general x54, matrix products, times_transposed(): lax.dot_general(left, right, (((1,), (1,)), ((), ())), preferred_element_...  106 us
    dot_general x38, matrix products, outer_sum(): lax.dot_general(left, right, (((0,), (0,)), ((), ())), preferred_element_...  96.5 us
    unnamed x2, blocking collectives  89.8 us
    all_gather x1, waiting for transfers between devices, on_device(): lax.all_gather(w_down.astype(jnp.bfloat16), 'fsdp', axis=0, tiled=True)  87.4 us
    dot_general x38, matrix products, matmul(): return jnp.dot(left, right, preferred_element_type=jnp.float32)  74.9 us
  transfers between devices with their start and end apart: 20, of which 12 were waited for; matrix products, arithmetic and copies ran while one was open for 16% of the time, Pallas kernels for 0%

commit v1 on v0

--- a/solution.py
+++ b/solution.py
@@ -121,7 +121,12 @@
         lax.all_gather(ln2_bias.astype(jnp.bfloat16), "fsdp", axis=0, tiled=True),
         lax.all_gather(w_up.astype(jnp.bfloat16), "fsdp", axis=0, tiled=True),
         lax.all_gather(b_up.astype(jnp.bfloat16), "fsdp", axis=0, tiled=True),
-        lax.all_gather(w_down.astype(jnp.bfloat16), "fsdp", axis=0, tiled=True),
+        jnp.concatenate(
+            lax.all_to_all(
+                jnp.stack([w_down.astype(jnp.bfloat16)] * lax.axis_size("fsdp")), "fsdp", 0, 0
+            ),
+            axis=0,
+        ),
         lax.all_gather(b_down.astype(jnp.bfloat16), "fsdp", axis=0, tiled=True),
     )
     device_index = lax.axis_index("fsdp")

time: 1660 us -> 1850 us (1.11)
  waiting for transfers between devices: 1050 us -> 1150 us
  blocking collectives: 89.8 us -> 161 us
    all_to_all x0 -> x1, waiting for transfers between devices: none -> 341 us  [on_device(): lax.all_to_all(jnp.stack([w_down.astype(jnp.bfloat16)] * lax.axis_size('f...]
    reduce_scatter x1, waiting for transfers between devices: 472 us -> 217 us  [on_device(): lax.psum_scatter(jnp.concatenate([jnp.concatenate([outer_sum(normed, grad...]
    unnamed x2, blocking collectives: 89.8 us -> 161 us
  transfers between devices with their start and end apart: 20 -> 21, of which waited for: 12 -> 13; matrix products, arithmetic and copies ran while one was open for 16% -> 15% of each run, Pallas kernels for 0% -> 0%
where the time goes in v1:
time: 1850 us; the launch traced here: 1840 us
  waiting for transfers between devices  1150 us (62%)
  matrix products  278 us (15%)
  blocking collectives  161 us (9%)
  local copies, waits for them, and re-layouts  113 us (6%)
  other arithmetic  101 us (5%)
    all_to_all x1, waiting for transfers between devices, on_device(): lax.all_to_all(jnp.stack([w_down.astype(jnp.bfloat16)] * lax.axis_size('f...  341 us
    reduce_scatter x1, waiting for transfers between devices, on_device(): lax.psum_scatter(outer_sum(activated, cotangent), 'fsdp', scatter_dimensi...  296 us
    reduce_scatter x1, waiting for transfers between devices, on_device(): lax.psum_scatter(jnp.concatenate([jnp.concatenate([outer_sum(normed, grad...  217 us
    unnamed x2, blocking collectives  161 us
    ppermute x12, waiting for transfers between devices, swapped(): return lax.ppermute(block, axis, route)  136 us
    dot_general x54, matrix products, times_transposed(): lax.dot_general(left, right, (((1,), (1,)), ((), ())), preferred_element_...  107 us
    dot_general x38, matrix products, outer_sum(): lax.dot_general(left, right, (((0,), (0,)), ((), ())), preferred_element_...  96.5 us
    all_gather x1, waiting for transfers between devices, on_device(): lax.all_gather(w_down.astype(jnp.bfloat16), 'fsdp', axis=0, tiled=True)  87.6 us
  transfers between devices with their start and end apart: 21, of which 13 were waited for; matrix products, arithmetic and copies ran while one was open for 15% of the time, Pallas kernels for 0%

profile of v1, /device:TPU:14, one launch (start us, length us, event | category | flops | bytes accessed | tf_op | source)
XLA Modules:
  0.0 1835.6 jit_solution(8402858360729319440)
XLA Ops:
  20.4 42.1 %all-reduce.19 = (bf16[1280]{0:T(1024)(128)(2,1)S(1)}, bf16[1280]{0:T(1024)(128)(2,1)S(1)}, bf16[1280]{0:T(1024)(128)(2,1)S(1)}, bf16[1280]{0:T(1024)(128)(2,1)S...) all-reduce(bf16[1280]{0:T(1024)(128)(2,1)S(1)} %dynamic-update-slic, ...), channel_id=1, replica_groups=mesh['fsdp'=32] {'fsdp'}, use_global_device_ids=true, to_apply=%add.2 | all-reduce | flops 15360 | bytes 61440
  63.0 7.7 all-gather.9.cloned.1.call-done
  73.8 58.2 %all-gather.11.cloned.1.call-done = bf16[1280,1280]{1,0:T(8,128)(2,1)} async-done(((bf16[40,1280]{1,0:T(8,128)(2,1)}), bf16[1280,1280]{1,0:T(8,128)(2,1)}) %all-gather.11.cloned.1.call-update) | async-done | bytes 3276816 | tf_op jit(solution)/shard_map/all_gather | solution.py:116
  139.2 22.8 %collective-permute-done.1 = bf16[384,1280]{1,0:T(8,128)(2,1)S(1)} collective-permute-done((bf16[384,1280]{1,0:T(8,128)(2,1)}, bf16[384,1280]{1,0:T(8,128)(2,1)S(1)}, u32[]{:S(2)}, u32[]{:S(2)}) %collective-permute-start.1) | collective-permute-done | bytes 983072 | tf_op jit(solution)/shard_map/ppermute | solution.py:22
  162.0 3.4 maximum_select_fusion.2
  167.2 22.2 %collective-permute-done.4 = bf16[384,1280]{1,0:T(8,128)(2,1)S(1)} collective-permute-done((bf16[384,1280]{1,0:T(8,128)(2,1)S(1)}, bf16[384,1280]{1,0:T(8,128)(2,1)S(1)}, u32[]{:S(2)}, u32[]{:S(2)}) %collective-permute-start.4) | collective-permute-done | bytes 983072 | tf_op jit(solution)/shard_map/ppermute | solution.py:22
  201.7 3.6 fusion.56
  211.9 4.2 maximum_select_fusion.7
  219.7 3.3 maximum_select_fusion.3
  223.5 4.1 copy.129
  227.6 5.7 fusion.47
  233.3 7.7 copy.138
  241.0 24.2 %collective-permute-done.5 = bf16[768,1280]{1,0:T(8,128)(2,1)} collective-permute-done((bf16[768,1280]{1,0:T(8,128)(2,1)}, bf16[768,1280]{1,0:T(8,128)(2,1)}, u32[]{:S(2)}, u32[]{:S(2)}) %collective-permute-start.5) | collective-permute-done | bytes 1966112 | tf_op jit(solution)/shard_map/ppermute | solution.py:22
  265.1 4.0 copy.133
  269.2 4.7 fusion.48
  273.9 7.8 copy.139
  281.8 84.0 %while.28 = (s32[]{:T(128)}, bf16[16,192,80]{1,2,0:T(8,128)(2,1)S(1)}, f32[16,192]{1,0:T(8,128)}, bf16[16,192,80]{2,1,0:T(8,128)(2,1)}, bf16[16,1536,80]{2,1,0:T...) while((s32[]{:T(128)}, ...), condition=%wide.region_5.6_spmd.clone, body=%wide.region_2.5_spmd.clone.sunk | while | flops 96732480 | bytes 4469869 | solution.py:181
  368.9 9.5 convolution_add_fusion
  378.4 87.6 %all-gather.17.cloned.1.call-done = bf16[5120,1280]{1,0:T(8,128)(2,1)} async-done(((bf16[160,1280]{1,0:T(8,128)(2,1)}), bf16[5120,1280]{1,0:T(8,128)(2,1)}) %all-gather.17.cloned.1.call-update) | async-done | bytes 13107216 | tf_op jit(solution)/shard_map/all_gather | solution.py:205
  466.0 17.3 convert_reduce_fusion
  483.3 10.1 multiply_reduce_fusion.1
  498.1 153.3 %while.29 = (s32[]{:T(128)}, bf16[16,192,80]{1,2,0:T(8,128)(2,1)S(1)}, f32[16,1536,80]{1,2,0:T(8,128)}, f32[16,1536,80]{1,2,0:T(8,128)}, bf16[16,192,80]{2,1,0:T...) while((s32[]{:T(128)}, ...), condition=%wide.region_12.13_spmd.clone, body=%wide.region_10.12_spmd.clone.sunk | while | flops 238723392 | bytes 11284349 | solution.py:238
  651.4 5.2 select_convert_fusion.1
  656.6 4.0 copy.145
  662.0 4.9 select_convert_fusion
  667.0 4.0 copy.147
  671.6 5.7 slice_select_fusion.1
  677.3 5.6 slice_select_fusion
  682.9 5.5 copy.146
  688.4 5.6 copy.148
  694.0 4.1 convolution_dynamic-update-slice_fusion.4
  698.1 8.5 collective-permute-done.6
  710.5 37.5 %collective-permute-done.9 = bf16[768,1280]{1,0:T(8,128)(2,1)} collective-permute-done((bf16[768,1280]{1,0:T(8,128)(2,1)}, bf16[768,1280]{1,0:T(8,128)(2,1)}, u32[]{:S(2)}, u32[]{:S(2)}) %collective-permute-start.9) | collective-permute-done | bytes 1966112 | tf_op jit(solution)/shard_map/ppermute | solution.py:22
  752.3 21.1 %collective-permute-done.10 = bf16[384,1280]{1,0:T(8,128)(2,1)S(1)} collective-permute-done((bf16[384,1280]{1,0:T(8,128)(2,1)S(1)}, bf16[384,1280]{1,0:T(8,128)(2,1)S(1)}, u32[]{:S(2)}, u32[]{:S(2)}) %collective-permute-start.10) | collective-permute-done | bytes 983072 | tf_op jit(solution)/shard_map/ppermute | solution.py:22
  774.1 4.1 convolution_dynamic-update-slice_fusion.3
  778.4 3.9 convolution_dynamic-update-slice_fusion.2
  782.4 3.8 convolution_dynamic-update-slice_fusion.1
  786.2 10.7 convolution_dynamic-update-slice_fusion
  797.0 3.9 multiply_convert_fusion.1
  800.9 11.2 fusion.87
  812.1 7.1 stack.2
  819.2 5.7 all-to-all-start
  826.5 4.3 fusion.86
  830.8 341.4 %all-to-all-done = bf16[32,160,1280]{2,1,0:T(8,128)(2,1)} async-done(((bf16[32,160,1280]{2,1,0:T(8,128)(2,1)}), bf16[32,160,1280]{2,1,0:T(8,128)(2,1)}, u32[]{:S(2)}, u32[]{:S(2)}) %all-to-all-start) | async-done | bytes 13107232 | tf_op jit(solution)/shard_map/all_to_all | solution.py:125
  1172.1 8.7 fusion.55
  1186.3 119.4 %all-reduce.18 = (f32[1280]{0:T(1024)S(1)}, f32[1280]{0:T(1024)S(1)}, f32[1280]{0:T(1024)S(1)}, f32[1280]{0:T(1024)S(1)}, f32[1280]{0:T(1024)S(1)}, /*index=5*/f...) all-reduce(f32[1280]{0:T(1024)S(1)} %get-tuple-element.224, ...), channel_id=2, replica_groups=mesh['fsdp'=32] {'fsdp'}, use_global_device_ids=true, to_apply=%region_16.17.clone | all-reduce | flops 15360 | bytes 122880
  1311.0 217.4 %reduce-scatter.3.cloned.1.call-done = f32[40,10240]{1,0:T(8,128)} async-done(((f32[1280,10240]{1,0:T(8,128)}), f32[40,10240]{1,0:T(8,128)}) %reduce-scatter.3.cloned.1.call-update) | async-done | bytes 1638416 | tf_op jit(solution)/shard_map/reduce_scatter | solution.py:272
  1532.6 296.0 %reduce-scatter.5.cloned.1.call-done = f32[160,1280]{1,0:T(8,128)} async-done(((f32[5120,1280]{1,0:T(8,128)}), f32[160,1280]{1,0:T(8,128)}) %reduce-scatter.5.cloned.1.call-update) | async-done | bytes 819216 | tf_op jit(solution)/shard_map/reduce_scatter | solution.py:213
  (442 shorter events, 320.6 us)
Async XLA Ops:
  7.2 11.0 copy-start.29
  7.2 11.0 copy-start.30
  7.2 11.0 copy-start.31
  7.2 11.0 copy-start.32
  7.2 11.0 copy-start.33
  7.2 11.0 copy-start.34
  7.3 11.0 copy-start.35
  7.3 11.1 copy-start.28
  7.3 11.1 copy-start.36
  7.3 55.3 %copy-start = (bf16[192,1280]{1,0:T(8,128)(2,1)S(1)}, bf16[192,1280]{1,0:T(8,128)(2,1)}, u32[]{:S(2)}) copy-start(bf16[192,1280]{1,0:T(8,128)(2,1)} %param.22) | copy-start | bytes 1474564
  7.3 63.4 %all-gather.9.cloned.1.call-start = ((), (), s32[]{:S(2)}) async-start(), calls=%async_computation.4 | async-start | bytes 3379200 | tf_op jit(solution)/shard_map/all_gather | solution.py:115
  9.0 123.0 %all-gather.11.cloned.1.call-start = ((), (), s32[]{:S(2)}) async-start(), calls=%async_computation.5 | async-start | bytes 3379200 | tf_op jit(solution)/shard_map/all_gather | solution.py:116
  10.7 191.0 %all-gather.7.cloned.1.call-start = ((), (), s32[]{:S(2)}) async-start(), calls=%async_computation.3 | async-start | bytes 3379200 | tf_op jit(solution)/shard_map/all_gather | solution.py:113
  12.3 353.4 %all-gather.13.cloned.1.call-start = ((), (), s32[]{:S(2)}) async-start(), calls=%async_computation.6 | async-start | bytes 3379200 | tf_op jit(solution)/shard_map/all_gather | solution.py:118
  14.0 354.9 %all-gather.15.cloned.1.call-start = ((), (), s32[]{:S(2)}) async-start(), calls=%async_computation.7 | async-start | bytes 13516800 | tf_op jit(solution)/shard_map/all_gather | solution.py:122
  16.1 450.0 %all-gather.17.cloned.1.call-start = ((), (), s32[]{:S(2)}) async-start(), calls=%async_computation.8 | async-start | bytes 13516800 | tf_op jit(solution)/shard_map/all_gather | solution.py:205
  18.1 1510.3 %reduce-scatter.3.cloned.1.call-start = ((), (), s32[]{:S(2)}) async-start(), calls=%async_computation.9 | async-start | bytes 54067200 | tf_op jit(solution)/shard_map/reduce_scatter | solution.py:272
  63.0 71.8 %copy-start.25 = (f32[192]{0:T(256)}, f32[192]{0:T(256)S(1)}, u32[]{:S(2)}) copy-start(f32[192]{0:T(256)S(1)} %fusion.67) | copy-start | bytes 2308
  73.5 64.4 %copy-start.21 = (bf16[192,1280]{1,0:T(8,128)(2,1)}, bf16[192,1280]{1,0:T(8,128)(2,1)S(1)}, u32[]{:S(2)}) copy-start(bf16[192,1280]{1,0:T(8,128)(2,1)S(1)} %convolution_convert_fusion.1) | copy-start | bytes 1474564
  73.5 61.6 %collective-permute-start = (bf16[192,1280]{1,0:T(8,128)(2,1)S(1)}, bf16[192,1280]{1,0:T(8,128)(2,1)S(1)}, u32[]{:S(2)}, u32[]{:S(2)}) collective-permute-start(bf16[192,1280]{1,0:T(8,128)(2,1)S(1)} %convolution_convert_fusion.1), channel_id=1, source_target_pairs={{0,1},{1,0},{2,3},{3,2},{4,5},{5,4},{6,7},{7,6},{8,9},{9,8},{10,11... | collective-permute-start | bytes 1474568 | tf_op jit(solution)/shard_map/ppermute | solution.py:22
  134.8 3.0 collective-permute-start.3
  136.4 25.6 %collective-permute-start.1 = (bf16[384,1280]{1,0:T(8,128)(2,1)}, bf16[384,1280]{1,0:T(8,128)(2,1)S(1)}, u32[]{:S(2)}, u32[]{:S(2)}) collective-permute-start(bf16[384,1280]{1,0:T(8,128)(2,1)} %maximum_select_fusion.6), channel_id=1, source_target_pairs={{0,2},{2,0},{1,3},{3,1},{4,6},{6,4},{5,7},{7,5},{8,10},{10,8},{9,1... | collective-permute-start | bytes 2949128 | tf_op jit(solution)/shard_map/ppermute | solution.py:22
  138.7 50.7 %collective-permute-start.4 = (bf16[384,1280]{1,0:T(8,128)(2,1)S(1)}, bf16[384,1280]{1,0:T(8,128)(2,1)S(1)}, u32[]{:S(2)}, u32[]{:S(2)}) collective-permute-start(bf16[384,1280]{1,0:T(8,128)(2,1)S(1)} %maximum_select_fusion.8), channel_id=1, source_target_pairs={{0,2},{2,0},{1,3},{3,1},{4,6},{6,4},{5,7},{7,5},{8,10},{10,8},{9,1... | collective-permute-start | bytes 2949128 | tf_op jit(solution)/shard_map/ppermute | solution.py:22
  139.2 54.4 %copy-start.37 = (s32[4]{0:T(128)S(1)}, s32[4]{0:T(128)}, u32[]{:S(2)}) copy-start(s32[4]{0:T(128)} %param.38) | copy-start | bytes 52
  165.4 58.1 %collective-permute-start.2 = (bf16[768,1280]{1,0:T(8,128)(2,1)}, bf16[768,1280]{1,0:T(8,128)(2,1)}, u32[]{:S(2)}, u32[]{:S(2)}) collective-permute-start(bf16[768,1280]{1,0:T(8,128)(2,1)} %maximum_select_fusion.2), channel_id=1, source_target_pairs={{0,4},{4,0},{1,5},{5,1},{2,6},{6,2},{3,7},{7,3},{8,12},{12,8},{9,1... | collective-permute-start | bytes 5898248 | tf_op jit(solution)/shard_map/ppermute | solution.py:22
  189.3 15.9 copy-start.14
  191.3 73.8 %collective-permute-start.5 = (bf16[768,1280]{1,0:T(8,128)(2,1)}, bf16[768,1280]{1,0:T(8,128)(2,1)}, u32[]{:S(2)}, u32[]{:S(2)}) collective-permute-start(bf16[768,1280]{1,0:T(8,128)(2,1)} %maximum_select_fusion.4), channel_id=1, source_target_pairs={{0,4},{4,0},{1,5},{5,1},{2,6},{6,2},{3,7},{7,3},{8,12},{12,8},{9,1... | collective-permute-start | bytes 5898248 | tf_op jit(solution)/shard_map/ppermute | solution.py:22
  368.9 97.1 %copy-start.7 = (bf16[192,1280]{1,0:T(8,128)(2,1)S(1)}, bf16[192,1280]{1,0:T(8,128)(2,1)}, u32[]{:S(2)}) copy-start(bf16[192,1280]{1,0:T(8,128)(2,1)} %param.39) | copy-start | bytes 1474564
  483.3 10.1 copy-start.18
  651.4 42.6 %copy-start.6 = (bf16[16,192,80]{1,2,0:T(8,128)(2,1)}, bf16[16,192,80]{1,2,0:T(8,128)(2,1)S(1)}, u32[]{:S(2)}) copy-start(bf16[16,192,80]{1,2,0:T(8,128)(2,1)S(1)} %get-tuple-element.111) | copy-start | bytes 1474564
  660.6 46.0 %collective-permute-start.6 = (bf16[768,1280]{1,0:T(8,128)(2,1)}, bf16[768,1280]{1,0:T(8,128)(2,1)}, u32[]{:S(2)}, u32[]{:S(2)}) collective-permute-start(bf16[768,1280]{1,0:T(8,128)(2,1)} %copy.145), channel_id=1, source_target_pairs={{0,4},{4,0},{1,5},{5,1},{2,6},{6,2},{3,7},{7,3},{8,12},{12,8},{9,1... | collective-permute-start | bytes 5898248 | tf_op jit(solution)/shard_map/ppermute | solution.py:22
  671.0 77.0 %collective-permute-start.9 = (bf16[768,1280]{1,0:T(8,128)(2,1)}, bf16[768,1280]{1,0:T(8,128)(2,1)}, u32[]{:S(2)}, u32[]{:S(2)}) collective-permute-start(bf16[768,1280]{1,0:T(8,128)(2,1)} %copy.147), channel_id=1, source_target_pairs={{0,4},{4,0},{1,5},{5,1},{2,6},{6,2},{3,7},{7,3},{8,12},{12,8},{9,1... | collective-permute-start | bytes 5898248 | tf_op jit(solution)/shard_map/ppermute | solution.py:22
  694.0 12.6 copy-start.2
  706.6 41.4 %copy-start.1 = (f32[768,1280]{1,0:T(8,128)S(1)}, f32[768,1280]{1,0:T(8,128)}, u32[]{:S(2)}) copy-start(f32[768,1280]{1,0:T(8,128)} %copy.148) | copy-start | bytes 11796484
  709.0 42.8 %collective-permute-start.7 = (bf16[384,1280]{1,0:T(8,128)(2,1)S(1)}, bf16[384,1280]{1,0:T(8,128)(2,1)S(1)}, u32[]{:S(2)}, u32[]{:S(2)}) collective-permute-start(bf16[384,1280]{1,0:T(8,128)(2,1)S(1)} %select_convert_fusion.3), channel_id=1, source_target_pairs={{0,2},{2,0},{1,3},{3,1},{4,6},{6,4},{5,7},{7,5},{8,10},{10,8},{9,1... | collective-permute-start | bytes 2949128 | tf_op jit(solution)/shard_map/ppermute | solution.py:22
  750.3 23.1 %collective-permute-start.10 = (bf16[384,1280]{1,0:T(8,128)(2,1)S(1)}, bf16[384,1280]{1,0:T(8,128)(2,1)S(1)}, u32[]{:S(2)}, u32[]{:S(2)}) collective-permute-start(bf16[384,1280]{1,0:T(8,128)(2,1)S(1)} %select_convert_fusion.2), channel_id=1, source_target_pairs={{0,2},{2,0},{1,3},{3,1},{4,6},{6,4},{5,7},{7,5},{8,10},{10,8},{9,1... | collective-permute-start | bytes 2949128 | tf_op jit(solution)/shard_map/ppermute | solution.py:22
  752.2 21.8 %collective-permute-start.8 = (bf16[192,1280]{1,0:T(8,128)(2,1)S(1)}, bf16[192,1280]{1,0:T(8,128)(2,1)S(1)}, u32[]{:S(2)}, u32[]{:S(2)}) collective-permute-start(bf16[192,1280]{1,0:T(8,128)(2,1)S(1)} %select_convert_fusion.5), channel_id=1, source_target_pairs={{0,1},{1,0},{2,3},{3,2},{4,5},{5,4},{6,7},{7,6},{8,9},{9,8},{10,11... | collective-permute-start | bytes 1474568 | tf_op jit(solution)/shard_map/ppermute | solution.py:22
  773.9 4.4 collective-permute-start.11
  774.1 4.1 copy-start.12
  778.4 3.9 copy-start.10
  782.4 3.8 copy-start.19
  796.9 1031.7 %reduce-scatter.5.cloned.1.call-start = ((), (), s32[]{:S(2)}) async-start(), calls=%async_computation.10 | async-start | bytes 27033600 | tf_op jit(solution)/shard_map/reduce_scatter | solution.py:213
  797.0 3.9 copy-start.8
  819.2 5.7 copy-start.27
  819.2 352.9 %all-to-all-start = ((bf16[32,160,1280]{2,1,0:T(8,128)(2,1)}), bf16[32,160,1280]{2,1,0:T(8,128)(2,1)}, u32[]{:S(2)}, u32[]{:S(2)}) async-start(bf16[32,160,1280]{2,1,0:T(8,128)(2,1)} %stack.2), calls=%async_computation | async-start | bytes 26214400 | tf_op jit(solution)/shard_map/all_to_all | solution.py:125
  1172.1 8.7 copy-start.13
  1172.1 8.7 copy-start.16
  1172.1 8.7 copy-start.24
  (11 other events, 22.0 us)
Sparse Core Ops, SparseCore 0:
  11.5 59.1 all-gather.8
  74.1 57.8 all-gather.10
  135.4 66.1 all-gather.6
  204.9 63.4 all-gather.12
  271.1 95.7 all-gather.14
  369.6 96.3 all-gather.16
  797.0 731.3 reduce-scatter.2
  1531.3 297.2 reduce-scatter.4
